TPU v7x, 32 devices: a whole 2x2x4 slice. The times are simulated.
32 devices in a mesh: fsdp: 8 (over z, y), ctx: 2 (over x), tp: 2 (over core).
Axes of the slice: x: 2, y: 2, z: 4, core: 2. Of those that a mesh axis runs over, the one named last changes fastest.
Arguments:
- inputs: bfloat16 [2, 16, 592, 1024], P(None, ('fsdp', 'tp'), 'ctx'), may hold values from -6 to 6
- cotangent: bfloat16 [2, 16, 592, 1024], P(None, ('fsdp', 'tp'), 'ctx'), may hold values from -6 to 6
- slot_mask: int32 [2, 16], P(None, ('fsdp', 'tp')), may hold values 0 or 1
- key_mask: int32 [2, 16, 592], P(None, 'fsdp'), may hold values from 0 to 1, as said below
- ln1_gain: bfloat16 [1024], P('fsdp'), may hold values from 0.5 to 1.5
- ln1_bias: bfloat16 [1024], P('fsdp'), may hold values from -0.796875 to 0.796875
- w_qkv: bfloat16 [1024, 3, 1024], P('fsdp', None, 'tp'), may hold values from -0.1875 to 0.1875
- b_qv: bfloat16 [2, 16, 64], P(None, 'tp', 'fsdp'), may hold values from -0.796875 to 0.796875
- w_out: bfloat16 [1024, 1024], P('tp', 'fsdp'), may hold values from -2.5 to 2.5
- b_out: bfloat16 [1024], P('fsdp'), may hold values from -0.796875 to 0.796875
- ln2_gain: bfloat16 [1024], P('fsdp'), may hold values from 0.5 to 1.5
- ln2_bias: bfloat16 [1024], P('fsdp'), may hold values from -0.796875 to 0.796875
- w_fc1: bfloat16 [1024, 4096], P('fsdp', 'tp'), may hold values from -0.1875 to 0.1875
- b_fc1: bfloat16 [64, 64], P('tp', 'fsdp'), may hold values from -0.796875 to 0.796875
- w_fc2: bfloat16 [4096, 1024], P('tp', 'fsdp'), may hold values from -0.09375 to 0.09375
- b_fc2: bfloat16 [1024], P('fsdp'), may hold values from -0.796875 to 0.796875
Outputs:
- outputs: bfloat16 [2, 16, 592, 1024], P(None, ('fsdp', 'tp'), 'ctx')
- input_grad: bfloat16 [2, 16, 592, 1024], P(None, ('fsdp', 'tp'), 'ctx')
- ln1_gain_grad: float32 [1024], P(('fsdp', 'ctx', 'tp'))
- ln1_bias_grad: float32 [1024], P(('fsdp', 'ctx', 'tp'))
- w_qkv_grad: float32 [1024, 3, 1024], P(('fsdp', 'ctx'), None, 'tp')
- b_qv_grad: float32 [2, 16, 64], P(None, 'tp', ('fsdp', 'ctx'))
- w_out_grad: float32 [1024, 1024], P('tp', ('fsdp', 'ctx'))
- b_out_grad: float32 [1024], P(('fsdp', 'ctx', 'tp'))
- ln2_gain_grad: float32 [1024], P(('fsdp', 'ctx', 'tp'))
- ln2_bias_grad: float32 [1024], P(('fsdp', 'ctx', 'tp'))
- w_fc1_grad: float32 [1024, 4096], P(('fsdp', 'ctx'), 'tp')
- b_fc1_grad: float32 [64, 64], P('tp', ('fsdp', 'ctx'))
- w_fc2_grad: float32 [4096, 1024], P('tp', ('fsdp', 'ctx'))
- b_fc2_grad: float32 [1024], P(('fsdp', 'ctx', 'tp'))
Inputs may be any that keep to these rules, and one draw needn't show every extreme that they name: `key_mask`: position 0 of every image is 1; positions 577 and beyond are 0.
All inputs are finite; a program needn't handle non-finite values. No bound on the sum of `slot_mask` on one device may be relied on, other than what follows from the above.
Results may differ from a plain program's by a relative error of at most 0.023.
Values may be sent and summed in bfloat16 or wider, within the bound.
A program may use at most 256 MiB of HBM per device.

v0:
```python
import jax
import jax.numpy as jnp
from jax import lax
from jax.sharding import PartitionSpec as P

HD = 64
SEQ_LEN = 577


def normalize_rows(values, gain_row, shift_row):
    average = jnp.mean(values, axis=-1, keepdims=True)
    centred = values - average
    inv_std = lax.rsqrt(jnp.mean(centred * centred, axis=-1, keepdims=True) + 1e-05)
    normed = centred * inv_std
    return (normed, inv_std, normed * gain_row + shift_row)


def normalize_back(upstream, normed, inv_std, gain_row):
    scaled = upstream * gain_row
    inner_term = (
        scaled
        - jnp.mean(scaled, axis=-1, keepdims=True)
        - normed * jnp.mean(scaled * normed, axis=-1, keepdims=True)
    )
    return inv_std * inner_term


def masked_scores(query_heads, key_heads, valid_keys):
    scores = (
        jnp.einsum("gqhd,gkhd->ghqk", query_heads, key_heads, preferred_element_type=jnp.float32)
        * 0.125
    )
    return jnp.where(valid_keys[:, None, None, :], scores, -jnp.inf)


def row_product(source, weight, einsum_form):
    return jnp.einsum(einsum_form, source, weight, preferred_element_type=jnp.float32)


def body(
    inputs,
    cotangent,
    slot_mask,
    key_mask,
    ln1_gain,
    ln1_bias,
    w_qkv,
    b_qv,
    w_out,
    b_out,
    ln2_gain,
    ln2_bias,
    w_fc1,
    b_fc1,
    w_fc2,
    b_fc2,
):
    gathered = (
        lax.all_gather(ln1_gain, "fsdp", axis=0, tiled=True),
        lax.all_gather(ln1_bias, "fsdp", axis=0, tiled=True),
        lax.all_gather(ln2_gain, "fsdp", axis=0, tiled=True),
        lax.all_gather(ln2_bias, "fsdp", axis=0, tiled=True),
        lax.all_gather(b_out, "fsdp", axis=0, tiled=True),
        lax.all_gather(b_fc2, "fsdp", axis=0, tiled=True),
        lax.all_gather(w_qkv, "fsdp", axis=0, tiled=True),
        lax.all_gather(b_qv, "fsdp", axis=2, tiled=True),
        lax.all_gather(w_out, "fsdp", axis=1, tiled=True),
        lax.all_gather(w_fc1, "fsdp", axis=0, tiled=True),
        lax.all_gather(b_fc1, "fsdp", axis=1, tiled=True),
        lax.all_gather(w_fc2, "fsdp", axis=1, tiled=True),
    )
    gain_one = gathered[0].astype(jnp.float32)
    shift_one = gathered[1].astype(jnp.float32)
    gain_two = gathered[2].astype(jnp.float32)
    shift_two = gathered[3].astype(jnp.float32)
    bias_out = gathered[4].astype(jnp.float32)
    bias_fc2 = gathered[5].astype(jnp.float32)
    matrices = (gathered[6], gathered[7], gathered[8], gathered[9], gathered[10], gathered[11])
    qkv_weight = matrices[0]
    bias_qv = matrices[1].reshape(2, -1).astype(jnp.float32)
    out_weight = matrices[2]
    fc1_weight = matrices[3]
    bias_fc1 = matrices[4].reshape(-1).astype(jnp.float32)
    fc2_weight = matrices[5]
    micro_count, own_images, own_tokens, model_width = inputs.shape
    heads_local = qkv_weight.shape[2] // HD
    position = lax.axis_index("ctx") * own_tokens + jnp.arange(own_tokens)
    position_ok = position < SEQ_LEN
    acc_qkv = jnp.zeros(qkv_weight.shape, jnp.float32)
    acc_bias_qv = jnp.zeros((2, heads_local * HD), jnp.float32)
    acc_out = jnp.zeros(out_weight.shape, jnp.float32)
    acc_fc1 = jnp.zeros(fc1_weight.shape, jnp.float32)
    acc_bias_fc1 = jnp.zeros(bias_fc1.shape, jnp.float32)
    acc_fc2 = jnp.zeros(fc2_weight.shape, jnp.float32)
    vector_sums = [jnp.zeros((model_width,), jnp.float32) for column in range(6)]
    output_list = []
    input_list = []
    for micro_step in range(micro_count):
        rows_in = inputs[micro_step].astype(jnp.float32)
        valid_rows = ((slot_mask[micro_step] > 0)[:, None] & position_ok[None, :]).astype(
            jnp.float32
        )[:, :, None]
        normed_one, inv_one, scaled_one = normalize_rows(rows_in, gain_one, shift_one)
        group_rows = lax.all_gather(scaled_one.astype(jnp.bfloat16), "tp", axis=0, tiled=True)
        valid_keys = key_mask[micro_step] > 0
        group_size = group_rows.shape[0]
        joint_proj = jnp.einsum(
            "gcd,dke->gcke", group_rows, qkv_weight, preferred_element_type=jnp.float32
        )
        query_own = (joint_proj[:, :, 0] + bias_qv[0]).astype(jnp.bfloat16)
        key_own = joint_proj[:, :, 1].astype(jnp.bfloat16)
        value_own = (joint_proj[:, :, 2] + bias_qv[1]).astype(jnp.bfloat16)
        key_all, value_all = (
            lax.all_gather(key_own, "ctx", axis=1, tiled=True),
            lax.all_gather(value_own, "ctx", axis=1, tiled=True),
        )
        query_heads = query_own.reshape(group_size, own_tokens, heads_local, HD)
        key_heads = key_all.reshape(group_size, -1, heads_local, HD)
        value_heads = value_all.reshape(group_size, -1, heads_local, HD)
        scores = masked_scores(query_heads, key_heads, valid_keys)
        row_max = jnp.max(scores, axis=-1, keepdims=True)
        lifted = jnp.exp(scores - row_max)
        row_sum = jnp.sum(lifted, axis=-1, keepdims=True)
        log_total = row_max + jnp.log(row_sum)
        attention = (lifted / row_sum).astype(jnp.bfloat16)
        mixed_heads = jnp.einsum(
            "ghqk,gkhd->gqhd", attention, value_heads, preferred_element_type=jnp.float32
        )
        mixed_heads = mixed_heads.reshape(group_size, own_tokens, -1).astype(jnp.bfloat16)
        attn_out = lax.psum_scatter(
            row_product(mixed_heads, out_weight, "gce,ed->gcd").astype(jnp.bfloat16),
            "tp",
            scatter_dimension=0,
            tiled=True,
        ).astype(jnp.float32)
        hidden_one = rows_in + attn_out + bias_out
        normed_two, inv_two, scaled_two = normalize_rows(hidden_one, gain_two, shift_two)
        group_two = lax.all_gather(scaled_two.astype(jnp.bfloat16), "tp", axis=0, tiled=True)
        before = (
            jnp.einsum("gcd,df->gcf", group_two, fc1_weight, preferred_element_type=jnp.float32)
            + bias_fc1
        )
        gate_sig = jax.nn.sigmoid(1.702 * before)
        active = (before * gate_sig).astype(jnp.bfloat16)
        mlp_out = lax.psum_scatter(
            row_product(active, fc2_weight, "gcf,fd->gcd").astype(jnp.bfloat16),
            "tp",
            scatter_dimension=0,
            tiled=True,
        ).astype(jnp.float32)
        output_list.append(((hidden_one + mlp_out + bias_fc2) * valid_rows).astype(jnp.bfloat16))
        again = (
            lax.all_gather(ln1_gain, "fsdp", axis=0, tiled=True),
            lax.all_gather(ln2_gain, "fsdp", axis=0, tiled=True),
            lax.all_gather(w_qkv, "fsdp", axis=0, tiled=True),
            lax.all_gather(w_out, "fsdp", axis=1, tiled=True),
            lax.all_gather(w_fc1, "fsdp", axis=0, tiled=True),
            lax.all_gather(w_fc2, "fsdp", axis=1, tiled=True),
        )
        back_gain_one = again[0].astype(jnp.float32)
        back_gain_two = again[1].astype(jnp.float32)
        back_mats = (again[2], again[3], again[4], again[5])
        back_qkv = back_mats[0]
        back_out = back_mats[1]
        back_fc1 = back_mats[2]
        back_fc2 = back_mats[3]
        grad_out = cotangent[micro_step].astype(jnp.float32) * valid_rows
        vector_sums[5] = vector_sums[5] + jnp.sum(grad_out, axis=(0, 1))
        group_grad = lax.all_gather(grad_out.astype(jnp.bfloat16), "tp", axis=0, tiled=True)
        acc_fc2 = acc_fc2 + jnp.einsum(
            "gcf,gcd->fd", active, group_grad, preferred_element_type=jnp.float32
        )
        grad_active = jnp.einsum(
            "gcd,fd->gcf", group_grad, back_fc2, preferred_element_type=jnp.float32
        )
        grad_before = (
            grad_active * (gate_sig + 1.702 * before * gate_sig * (1.0 - gate_sig))
        ).astype(jnp.bfloat16)
        acc_bias_fc1 = acc_bias_fc1 + jnp.sum(grad_before, axis=(0, 1), dtype=jnp.float32)
        acc_fc1 = acc_fc1 + jnp.einsum(
            "gcd,gcf->df", group_two, grad_before, preferred_element_type=jnp.float32
        )
        grad_two = lax.psum_scatter(
            row_product(grad_before, back_fc1, "gcf,df->gcd").astype(jnp.bfloat16),
            "tp",
            scatter_dimension=0,
            tiled=True,
        ).astype(jnp.float32)
        vector_sums[2] = vector_sums[2] + jnp.sum(grad_two * normed_two, axis=(0, 1))
        vector_sums[3] = vector_sums[3] + jnp.sum(grad_two, axis=(0, 1))
        grad_hidden = grad_out + normalize_back(grad_two, normed_two, inv_two, back_gain_two)
        vector_sums[4] = vector_sums[4] + jnp.sum(grad_hidden, axis=(0, 1))
        group_hidden = lax.all_gather(grad_hidden.astype(jnp.bfloat16), "tp", axis=0, tiled=True)
        acc_out = acc_out + jnp.einsum(
            "gce,gcd->ed", mixed_heads, group_hidden, preferred_element_type=jnp.float32
        )
        grad_mixed = jnp.einsum(
            "gcd,ed->gce", group_hidden, back_out, preferred_element_type=jnp.float32
        ).astype(jnp.bfloat16)
        grad_mixed = grad_mixed.reshape(group_size, own_tokens, heads_local, HD)
        scores_again = masked_scores(query_heads, key_heads, valid_keys)
        soft_again = jnp.exp(scores_again - log_total)
        grad_soft = jnp.einsum(
            "gqhd,gkhd->ghqk", grad_mixed, value_heads, preferred_element_type=jnp.float32
        )
        inner_sum = jnp.sum(grad_soft * soft_again, axis=-1, keepdims=True)
        grad_scores = (soft_again * (grad_soft - inner_sum)).astype(jnp.bfloat16)
        grad_query = (
            jnp.einsum(
                "ghqk,gkhd->gqhd", grad_scores, key_heads, preferred_element_type=jnp.float32
            )
            * 0.125
        ).astype(jnp.bfloat16)
        key_part = (
            jnp.einsum(
                "ghqk,gqhd->gkhd", grad_scores, query_heads, preferred_element_type=jnp.float32
            )
            * 0.125
        )
        value_part = jnp.einsum(
            "ghqk,gqhd->gkhd",
            soft_again.astype(jnp.bfloat16),
            grad_mixed,
            preferred_element_type=jnp.float32,
        )
        key_grad, value_grad = (
            lax.psum_scatter(
                key_part.reshape(group_size, -1, heads_local * HD).astype(jnp.bfloat16),
                "ctx",
                scatter_dimension=1,
                tiled=True,
            ).astype(jnp.float32),
            lax.psum_scatter(
                value_part.reshape(group_size, -1, heads_local * HD).astype(jnp.bfloat16),
                "ctx",
                scatter_dimension=1,
                tiled=True,
            ).astype(jnp.float32),
        )
        grad_joint = jnp.stack(
            [
                grad_query.reshape(group_size, own_tokens, -1),
                key_grad.astype(jnp.bfloat16),
                value_grad.astype(jnp.bfloat16),
            ],
            axis=2,
        )
        acc_bias_qv = acc_bias_qv + jnp.stack(
            [
                jnp.sum(grad_joint[:, :, 0], axis=(0, 1), dtype=jnp.float32),
                jnp.sum(grad_joint[:, :, 2], axis=(0, 1), dtype=jnp.float32),
            ]
        )
        acc_qkv = acc_qkv + jnp.einsum(
            "gcd,gcke->dke", group_rows, grad_joint, preferred_element_type=jnp.float32
        )
        grad_one = lax.psum_scatter(
            row_product(grad_joint, back_qkv, "gcke,dke->gcd").astype(jnp.bfloat16),
            "tp",
            scatter_dimension=0,
            tiled=True,
        ).astype(jnp.float32)
        vector_sums[0] = vector_sums[0] + jnp.sum(grad_one * normed_one, axis=(0, 1))
        vector_sums[1] = vector_sums[1] + jnp.sum(grad_one, axis=(0, 1))
        input_list.append(
            (grad_hidden + normalize_back(grad_one, normed_one, inv_one, back_gain_one)).astype(
                jnp.bfloat16
            )
        )
    grad_parts = (
        acc_qkv,
        acc_bias_qv.reshape(2, heads_local, HD),
        acc_out,
        acc_fc1,
        acc_bias_fc1.reshape(-1, 64),
        acc_fc2,
    )
    matrix_sums = (
        lax.psum_scatter(
            grad_parts[0].astype(jnp.bfloat16), ("fsdp", "ctx"), scatter_dimension=0, tiled=True
        ).astype(jnp.float32),
        lax.psum_scatter(
            grad_parts[1].astype(jnp.bfloat16), ("fsdp", "ctx"), scatter_dimension=2, tiled=True
        ).astype(jnp.float32),
        lax.psum_scatter(
            grad_parts[2].astype(jnp.bfloat16), ("fsdp", "ctx"), scatter_dimension=1, tiled=True
        ).astype(jnp.float32),
        lax.psum_scatter(
            grad_parts[3].astype(jnp.bfloat16), ("fsdp", "ctx"), scatter_dimension=0, tiled=True
        ).astype(jnp.float32),
        lax.psum_scatter(
            grad_parts[4].astype(jnp.bfloat16), ("fsdp", "ctx"), scatter_dimension=1, tiled=True
        ).astype(jnp.float32),
        lax.psum_scatter(
            grad_parts[5].astype(jnp.bfloat16), ("fsdp", "ctx"), scatter_dimension=1, tiled=True
        ).astype(jnp.float32),
    )
    vector_part = lax.psum_scatter(
        jnp.stack(vector_sums), ("fsdp", "ctx", "tp"), scatter_dimension=1, tiled=True
    )
    return (
        jnp.stack(output_list),
        jnp.stack(input_list),
        vector_part[0],
        vector_part[1],
        matrix_sums[0],
        matrix_sums[1],
        matrix_sums[2],
        vector_part[4],
        vector_part[2],
        vector_part[3],
        matrix_sums[3],
        matrix_sums[4],
        matrix_sums[5],
        vector_part[5],
    )


def solution(mesh):
    in_specs = (
        P(None, ("fsdp", "tp"), "ctx", None),
        P(None, ("fsdp", "tp"), "ctx", None),
        P(None, ("fsdp", "tp")),
        P(None, "fsdp", None),
        P("fsdp"),
        P("fsdp"),
        P("fsdp", None, "tp"),
        P(None, "tp", "fsdp"),
        P("tp", "fsdp"),
        P("fsdp"),
        P("fsdp"),
        P("fsdp"),
        P("fsdp", "tp"),
        P("tp", "fsdp"),
        P("tp", "fsdp"),
        P("fsdp"),
    )
    out_specs = (
        P(None, ("fsdp", "tp"), "ctx", None),
        P(None, ("fsdp", "tp"), "ctx", None),
        P(("fsdp", "ctx", "tp")),
        P(("fsdp", "ctx", "tp")),
        P(("fsdp", "ctx"), None, "tp"),
        P(None, "tp", ("fsdp", "ctx")),
        P("tp", ("fsdp", "ctx")),
        P(("fsdp", "ctx", "tp")),
        P(("fsdp", "ctx", "tp")),
        P(("fsdp", "ctx", "tp")),
        P(("fsdp", "ctx"), "tp"),
        P("tp", ("fsdp", "ctx")),
        P("tp", ("fsdp", "ctx")),
        P(("fsdp", "ctx", "tp")),
    )
    return jax.shard_map(body, mesh=mesh, in_specs=in_specs, out_specs=out_specs, check_vma=False)
```

profile of v0, /device:TPU:0, one launch (start us, length us, event | category | flops | bytes accessed | tf_op | source)
XLA Modules:
  0.0 1203.3 jit_solution(1417948135517288823)
XLA Ops:
  7.2 22.5 %all-gather.2 = bf16[8,1,128]{2,1,0:T(2,128)(2,1)S(1)} all-gather(bf16[1,1,128]{2,1,0:T(2,128)(2,1)} %bitcast.462), channel_id=1, replica_groups=mesh['fsdp'=8,'ctx'=2,'tp'=2] {'fsdp'}, dimensions={0}, use_global_device_ids=true | all-gather | bytes 2304 | tf_op jit(solution)/shard_map/all_gather | solution.py:59
  29.7 16.4 %all-gather.3 = bf16[8,1,128]{2,1,0:T(2,128)(2,1)S(1)} all-gather(bf16[1,1,128]{2,1,0:T(2,128)(2,1)} %bitcast.463), channel_id=1, replica_groups=mesh['fsdp'=8,'ctx'=2,'tp'=2] {'fsdp'}, dimensions={0}, use_global_device_ids=true | all-gather | bytes 2304 | tf_op jit(solution)/shard_map/all_gather | solution.py:60
  58.3 63.9 %all-gather.27.cloned.1.call-done = bf16[1024,3,512]{2,0,1:T(8,128)(2,1)} async-done(((bf16[128,3,512]{2,0,1:T(8,128)(2,1)}), bf16[1024,3,512]{2,0,1:T(8,128)(2,1)}) %all-gather.27.cloned.1.call-update) | async-done | bytes 3145744 | tf_op jit(solution)/shard_map/all_gather | solution.py:65
  129.4 30.4 %all_gather.88 = bf16[2,8,64]{1,0,2:T(2,128)(2,1)S(1)} all-gather(bf16[2,8,8]{1,0,2:T(2,128)(2,1)S(1)} %copy.164), channel_id=1, replica_groups=mesh['fsdp'=8,'ctx'=2,'tp'=2] {'fsdp'}, dimensions={2}, use_global_device_ids=true | all-gather | bytes 2304 | tf_op jit(solution)/shard_map/all_gather | solution.py:66
  199.5 31.7 %all-gather.31.cloned.1.call-done = bf16[512,1024]{1,0:T(8,128)(2,1)} async-done(((bf16[512,128]{1,0:T(8,128)(2,1)}), bf16[512,1024]{1,0:T(8,128)(2,1)}) %all-gather.31.cloned.1.call-update) | async-done | bytes 1048592 | tf_op jit(solution)/shard_map/all_gather | solution.py:67
  234.9 19.9 %all-gather.53.cloned.1.call-done = bf16[2,592,1,512]{3,1,2,0:T(8,128)(2,1)} async-done(((bf16[2,296,1,512]{3,1,2,0:T(8,128)(2,1)}), bf16[2,592,1,512]{3,1,2,0:T(8,128)(2,1)}) %all-gather.53.cloned.1.call-update) | async-done | bytes 1212432 | tf_op jit(solution)/shard_map/all_gather | solution.py:114
  268.9 10.7 all-gather.29.cloned.1.call-done
  291.6 20.4 %all-gather.4 = bf16[8,1,128]{2,1,0:T(2,128)(2,1)S(1)} all-gather(bf16[1,1,128]{2,1,0:T(2,128)(2,1)S(1)} %bitcast.464), channel_id=1, replica_groups=mesh['fsdp'=8,'ctx'=2,'tp'=2] {'fsdp'}, dimensions={0}, use_global_device_ids=true | all-gather | bytes 2304 | tf_op jit(solution)/shard_map/all_gather | solution.py:63
  312.0 16.4 %all-gather.5 = bf16[8,1,128]{2,1,0:T(2,128)(2,1)S(1)} all-gather(bf16[1,1,128]{2,1,0:T(2,128)(2,1)S(1)} %bitcast.465), channel_id=1, replica_groups=mesh['fsdp'=8,'ctx'=2,'tp'=2] {'fsdp'}, dimensions={0}, use_global_device_ids=true | all-gather | bytes 2304 | tf_op jit(solution)/shard_map/all_gather | solution.py:61
  328.4 18.3 %all-gather.6 = bf16[8,1,128]{2,1,0:T(2,128)(2,1)S(1)} all-gather(bf16[1,1,128]{2,1,0:T(2,128)(2,1)S(1)} %bitcast.466), channel_id=1, replica_groups=mesh['fsdp'=8,'ctx'=2,'tp'=2] {'fsdp'}, dimensions={0}, use_global_device_ids=true | all-gather | bytes 2304 | tf_op jit(solution)/shard_map/all_gather | solution.py:62
  357.3 26.5 %all_gather.97 = bf16[32,64]{0,1:T(8,128)(2,1)S(1)} all-gather(bf16[32,8]{0,1:T(8,128)(2,1)S(1)} %copy-done.45), channel_id=1, replica_groups=mesh['fsdp'=8,'ctx'=2,'tp'=2] {'fsdp'}, dimensions={1}, use_global_device_ids=true | all-gather | bytes 4608 | tf_op jit(solution)/shard_map/all_gather | solution.py:69
  402.4 78.1 %all-gather.37.cloned.1.call-done = bf16[2048,1024]{1,0:T(8,128)(2,1)} async-done(((bf16[2048,128]{1,0:T(8,128)(2,1)}), bf16[2048,1024]{1,0:T(8,128)(2,1)}) %all-gather.37.cloned.1.call-update) | async-done | bytes 4194320 | tf_op jit(solution)/shard_map/all_gather | solution.py:70
  480.5 8.8 convert_reduce_fusion
  502.2 8.8 convert_reduce_fusion.1
  531.8 20.4 %all-gather.7 = bf16[8,1,128]{2,1,0:T(2,128)(2,1)S(1)} all-gather(bf16[1,1,128]{2,1,0:T(2,128)(2,1)S(1)} %bitcast.467), channel_id=1, replica_groups=mesh['fsdp'=8,'ctx'=2,'tp'=2] {'fsdp'}, dimensions={0}, use_global_device_ids=true | all-gather | bytes 2304 | tf_op jit(solution)/shard_map/all_gather | solution.py:64
  656.6 21.4 %reduce-scatter.57.cloned.1.call-done = bf16[296,1024]{1,0:T(8,128)(2,1)} async-done(((bf16[592,1024]{1,0:T(8,128)(2,1)}), bf16[296,1024]{1,0:T(8,128)(2,1)}) %reduce-scatter.57.cloned.1.call-update) | async-done | bytes 606224
  696.9 8.7 fusion.4
  728.1 7.7 fusion.6
  738.9 43.9 %reduce-scatter.47.cloned.1.call-done = bf16[512,64]{0,1:T(8,128)(2,1)} async-done(((bf16[512,1024]{0,1:T(8,128)(2,1)}), bf16[512,64]{0,1:T(8,128)(2,1)}) %reduce-scatter.47.cloned.1.call-update) | async-done | bytes 65552 | tf_op jit(solution)/shard_map/reduce_scatter | solution.py:285
  785.8 73.3 %all-reduce.2 = (bf16[2,8,64]{1,0,2:T(2,128)(2,1)S(1)}, bf16[32,64]{1,0:T(8,128)(2,1)S(1)}) all-reduce(bf16[2,8,64]{1,0,2:T(2,128)(2,1)S(1)} %copy.187, bf16[32,64]{1,0:T(8,128)(2,1)S(1)} %convert_element_type.559), channel_id=18, replica_groups=mesh['fsdp'=8,'ctx'=2,'tp'=2] {'fsdp','ctx'}, use_global_device_ids=true, to_apply=%region_52.53.clone | all-reduce | flops 3072 | bytes 12288
  860.5 18.9 %reduce-scatter.51.cloned.1.call-done = bf16[2048,64]{0,1:T(8,128)(2,1)} async-done(((bf16[2048,1024]{0,1:T(8,128)(2,1)}), bf16[2048,64]{0,1:T(8,128)(2,1)}) %reduce-scatter.51.cloned.1.call-update) | async-done | bytes 262160 | tf_op jit(solution)/shard_map/reduce_scatter | solution.py:294
  881.1 95.2 %reduce-scatter.49.cloned.1.call-done = bf16[64,2048]{1,0:T(8,128)(2,1)} async-done(((bf16[1024,2048]{1,0:T(8,128)(2,1)}), bf16[64,2048]{1,0:T(8,128)(2,1)}) %reduce-scatter.49.cloned.1.call-update) | async-done | bytes 262160 | tf_op jit(solution)/shard_map/reduce_scatter | solution.py:288
  981.6 130.7 %reduce-scatter.61.cloned.1.call-done = f32[32,6]{1,0:T(8,128)} async-done(((f32[1024,6]{1,0:T(8,128)}), f32[32,6]{1,0:T(8,128)}) %reduce-scatter.61.cloned.1.call-update) | async-done | bytes 784
  1116.8 77.8 %reduce-scatter.45.cloned.1.call-done = bf16[64,3,512]{2,0,1:T(8,128)(2,1)} async-done(((bf16[1024,3,512]{2,0,1:T(8,128)(2,1)}), bf16[64,3,512]{2,0,1:T(8,128)(2,1)}) %reduce-scatter.45.cloned.1.call-update) | async-done | bytes 196624 | tf_op jit(solution)/shard_map/reduce_scatter | solution.py:279
  (372 shorter events, 314.6 us)
Async XLA Ops:
  50.3 71.9 %all-gather.27.cloned.1.call-start = ((), (), s32[]{:S(2)}) async-start(), calls=%async_computation.18 | async-start | bytes 3538944 | tf_op jit(solution)/shard_map/all_gather | solution.py:65
  51.0 109.0 %all-gather.25.cloned.1.call-start = ((), (), s32[]{:S(2)}) async-start(), calls=%async_computation.17 | async-start | bytes 1818624 | tf_op jit(solution)/shard_map/all_gather | solution.py:104
  51.7 125.4 %all-gather.55.cloned.1.call-start = ((), (), s32[]{:S(2)}) async-start(), calls=%async_computation.44 | async-start | bytes 1818624 | tf_op jit(solution)/shard_map/all_gather | solution.py:114
  129.2 61.9 %all-gather.41.cloned.1.call-start = ((), (), s32[]{:S(2)}) async-start(), calls=%async_computation.27 | async-start | bytes 1818624 | tf_op jit(solution)/shard_map/all_gather | solution.py:115
  167.9 63.4 %all-gather.31.cloned.1.call-start = ((), (), s32[]{:S(2)}) async-start(), calls=%async_computation.20 | async-start | bytes 1179648 | tf_op jit(solution)/shard_map/all_gather | solution.py:67
  168.5 86.4 %all-gather.53.cloned.1.call-start = ((), (), s32[]{:S(2)}) async-start(), calls=%async_computation.43 | async-start | bytes 1818624 | tf_op jit(solution)/shard_map/all_gather | solution.py:114
  170.7 108.8 %all-gather.29.cloned.1.call-start = ((), (), s32[]{:S(2)}) async-start(), calls=%async_computation.19 | async-start | bytes 1818624 | tf_op jit(solution)/shard_map/all_gather | solution.py:115
  176.8 169.9 %reduce-scatter.33.cloned.1.call-start = ((), (), s32[]{:S(2)}) async-start(), calls=%async_computation.28 | async-start | bytes 1818624 | tf_op jit(solution)/shard_map/reduce_scatter | solution.py:130
  234.3 112.3 %reduce-scatter.29.cloned.1.call-start = ((), (), s32[]{:S(2)}) async-start(), calls=%async_computation.21 | async-start | bytes 1818624 | tf_op jit(solution)/shard_map/reduce_scatter | solution.py:130
  290.8 93.2 %all-gather.35.cloned.1.call-start = ((), (), s32[]{:S(2)}) async-start(), calls=%async_computation.23 | async-start | bytes 4718592 | tf_op jit(solution)/shard_map/all_gather | solution.py:68
  291.5 98.8 %all-gather.43.cloned.1.call-start = ((), (), s32[]{:S(2)}) async-start(), calls=%async_computation.29 | async-start | bytes 1818624 | tf_op jit(solution)/shard_map/all_gather | solution.py:138
  355.5 125.0 %all-gather.37.cloned.1.call-start = ((), (), s32[]{:S(2)}) async-start(), calls=%async_computation.24 | async-start | bytes 4718592 | tf_op jit(solution)/shard_map/all_gather | solution.py:70
  356.1 138.7 %all-gather.33.cloned.1.call-start = ((), (), s32[]{:S(2)}) async-start(), calls=%async_computation.22 | async-start | bytes 1818624 | tf_op jit(solution)/shard_map/all_gather | solution.py:138
  356.7 145.5 %all-gather.45.cloned.1.call-start = ((), (), s32[]{:S(2)}) async-start(), calls=%async_computation.31 | async-start | bytes 1818624 | tf_op jit(solution)/shard_map/all_gather | solution.py:169
  357.3 194.9 %reduce-scatter.41.cloned.1.call-start = ((), (), s32[]{:S(2)}) async-start(), calls=%async_computation.36 | async-start | bytes 1818624 | tf_op jit(solution)/shard_map/reduce_scatter | solution.py:183
  565.4 71.7 %reduce-scatter.55.cloned.1.call-start = ((), (), s32[]{:S(2)}) async-start(), calls=%async_computation.46 | async-start | bytes 1818624
  610.8 67.3 %reduce-scatter.57.cloned.1.call-start = ((), (), s32[]{:S(2)}) async-start(), calls=%async_computation.47 | async-start | bytes 1818624
  631.1 93.2 %reduce-scatter.39.cloned.1.call-start = ((), (), s32[]{:S(2)}) async-start(), calls=%async_computation.34 | async-start | bytes 1818624 | tf_op jit(solution)/shard_map/reduce_scatter | solution.py:257
  648.2 76.1 %reduce-scatter.43.cloned.1.call-start = ((), (), s32[]{:S(2)}) async-start(), calls=%async_computation.38 | async-start | bytes 1818624 | tf_op jit(solution)/shard_map/reduce_scatter | solution.py:257
  685.7 97.0 %reduce-scatter.47.cloned.1.call-start = ((), (), s32[]{:S(2)}) async-start(), calls=%async_computation.40 | async-start | bytes 1114112 | tf_op jit(solution)/shard_map/reduce_scatter | solution.py:285
  690.4 188.9 %reduce-scatter.51.cloned.1.call-start = ((), (), s32[]{:S(2)}) async-start(), calls=%async_computation.42 | async-start | bytes 4456448 | tf_op jit(solution)/shard_map/reduce_scatter | solution.py:294
  705.7 270.6 %reduce-scatter.49.cloned.1.call-start = ((), (), s32[]{:S(2)}) async-start(), calls=%async_computation.41 | async-start | bytes 4456448 | tf_op jit(solution)/shard_map/reduce_scatter | solution.py:288
  716.8 395.5 %reduce-scatter.61.cloned.1.call-start = ((), (), s32[]{:S(2)}) async-start(), calls=%async_computation.49 | async-start | bytes 540672
  728.0 466.6 %reduce-scatter.45.cloned.1.call-start = ((), (), s32[]{:S(2)}) async-start(), calls=%async_computation.39 | async-start | bytes 3342336 | tf_op jit(solution)/shard_map/reduce_scatter | solution.py:279
  (77 other events, 1287.8 us)
Sparse Core Ops, SparseCore 0:
  60.5 61.6 all-gather.26
  133.6 24.2 all-gather.54
  168.0 21.7 all-gather.40
  191.7 39.5 all-gather.30
  232.8 22.0 all-gather.52
  256.4 23.1 all-gather.28
  293.8 9.8 reduce-scatter.28
  305.9 74.7 all-gather.34
  391.9 10.4 all-gather.48
  404.3 76.1 all-gather.36
  491.3 10.4 all-gather.44
  517.1 9.8 reduce-scatter.36
  541.3 9.8 reduce-scatter.34
  568.5 10.4 all-gather.50
  581.8 23.2 reduce-scatter.54
  607.3 22.1 reduce-scatter.52
  631.7 22.0 reduce-scatter.58
  655.9 22.1 reduce-scatter.56
  691.7 9.8 reduce-scatter.42
  703.9 78.7 reduce-scatter.46
  785.0 94.2 reduce-scatter.50
  881.7 94.5 reduce-scatter.48
  978.7 133.5 reduce-scatter.60
  1114.4 80.1 reduce-scatter.44
  (9 shorter events, 74.0 us)
where the time goes:
time: 1210 us; the launch traced here: 1200 us
  waiting for transfers between devices  616 us (51%)
  blocking collectives  245 us (20%)
  matrix products  189 us (16%)
  local copies, waits for them, and re-layouts  71.7 us (6%)
  other arithmetic  60 us (5%)
  between operations  18 us (1%)
    unnamed x38, waiting for transfers between devices  157 us
    reduce_scatter x1, waiting for transfers between devices, body(): lax.psum_scatter(grad_parts[3].astype(jnp.bfloat16), ('fsdp', 'ctx'), sca...  95.2 us
    all_gather x1, waiting for transfers between devices, body(): lax.all_gather(w_fc2, 'fsdp', axis=1, tiled=True)  78.1 us
    reduce_scatter x1, waiting for transfers between devices, body(): lax.psum_scatter(grad_parts[0].astype(jnp.bfloat16), ('fsdp', 'ctx'), sca...  77.8 us
    unnamed x1, blocking collectives  73.3 us
    all_gather x1, waiting for transfers between devices, body(): lax.all_gather(w_qkv, 'fsdp', axis=0, tiled=True)  63.9 us
    unnamed x161, local copies, waits for them, and re-layouts  49.1 us
    reduce_scatter x1, waiting for transfers between devices, body(): lax.psum_scatter(grad_parts[2].astype(jnp.bfloat16), ('fsdp', 'ctx'), sca...  43.9 us
  transfers between devices with their start and end apart: 33, of which 15 were waited for; matrix products, arithmetic and copies ran while one was open for 24% of the time, Pallas kernels for 0%

commit v1 on v0

v1 whole, which is shorter than its diff:
```python
import functools
import jax
import jax.numpy as jnp
from jax import lax
from jax.experimental import pallas as pl
from jax.experimental.pallas import tpu as pltpu
from jax.sharding import PartitionSpec as P

MESH = pl.DeviceIdType.MESH
BF = jnp.bfloat16
F32 = jnp.float32


class Place:
    def __init__(self, fsdp, ctx, tp):
        self.count, self.lines, self.tp_size = fsdp, fsdp // 2, tp
        self.fsdp = lax.axis_index("fsdp")
        self.line, self.pair = self.fsdp // 2, self.fsdp % 2
        self.half = lax.axis_index("ctx")
        self.core = lax.axis_index("tp")
        self.to_pair = {"fsdp": self.line * 2 + (1 - self.pair)}
        self.to_half = {"ctx": 1 - self.half}
        self.to_up = {"fsdp": self.fsdp + 2}
        self.to_down = {"fsdp": self.fsdp - 2}
        self.has_up = self.line < self.lines - 1
        self.has_down = self.line > 0

    def to_line(self, step):
        return {"fsdp": lax.rem(self.line + step, self.lines) * 2 + self.pair}

    def to_core(self, step):
        return {"tp": lax.rem(self.core + step, self.tp_size)}


def copy_to(src, dst, sems, slot, target):
    return pltpu.make_async_remote_copy(
        src_ref=src,
        dst_ref=dst,
        send_sem=sems[0].at[slot],
        recv_sem=sems[1].at[slot],
        device_id=target,
        device_id_type=MESH,
    )


def when(condition, action):
    if condition is True:
        action()
    else:
        pl.when(condition)(action)


class Gather:
    def __init__(self, place, pieces, sems, local_sems):
        self.place, self.pieces, self.sems, self.local_sems = place, pieces, sems, local_sems
        lines = place.lines
        names = ["first"]
        for kind in ("up", "down", "up_half", "down_half", "single_up", "single_down"):
            names += [(kind, step) for step in range(1, lines)]
        for kind in ("up_far", "down_far", "up_pair", "down_pair"):
            names += [(kind, step) for step in range(1, lines)]
        names += ["own_half", "own_pair", "up0a", "up0b", "down0a", "down0b"]
        names += [("core", step) for step in range(1, place.tp_size)]
        self.names = {name: number for number, name in enumerate(names)}
        self.width = len(names)
        self.pending = []

    @staticmethod
    def slots(lines, tp):
        return 1 + 10 * (lines - 1) + 6 + tp - 1

    def slot(self, piece, name):
        return piece * self.width + self.names[name]

    def whole(self, piece, core, line=slice(None), pair=slice(None), half=slice(None), color=slice(None)):
        _, ref, offset, width, per_core = self.pieces[piece]
        columns = pl.ds(pl.multiple_of(core * per_core + offset, 128), width)
        index = (line, pair, half, color, slice(None), columns)
        return ref.at[(slice(None),) * (len(ref.shape) - 6) + index]

    def own(self, piece, half=slice(None), color=slice(None)):
        ref, _, offset, width, _ = self.pieces[piece]
        index = (half, color, slice(None), pl.ds(offset, width))
        return ref.at[(slice(None),) * (len(ref.shape) - 4) + index]

    def send(self, piece, name, src, dst, target, condition=True):
        copy = copy_to(src, dst, self.sems, self.slot(piece, name), target)
        when(condition, copy.start)
        self.pending.append((copy, condition))

    def arrive(self, piece, name, dst, condition=True):
        copy = copy_to(dst, dst, self.sems, self.slot(piece, name), self.place.to_half)
        when(condition, copy.wait_recv)

    def local(self, piece):
        me = self.place
        return pltpu.make_async_copy(
            self.own(piece), self.whole(piece, me.core, me.line, me.pair), self.local_sems.at[piece]
        )

    def stage(self, p, k):
        me = self.place
        core, line, pair, half = me.core, me.line, me.pair, me.half
        lines = me.lines
        view = functools.partial(self.whole, p, core)
        if k == 0:
            self.local(p).start()
            self.send(p, "first", self.own(p, half, 0), view(line, pair, half, 0), me.to_pair)
            self.send(p, ("single_up", 1), self.own(p, half, 1), view(line, pair, half, 1), me.to_up, me.has_up)
            self.send(p, ("single_down", 1), self.own(p, half, 1), view(line, pair, half, 1), me.to_down, me.has_down)
            self.send(p, "up0a", self.own(p, half, 0), view(line, pair, half, 0), me.to_up, me.has_up)
            self.send(p, "down0a", self.own(p, half, 0), view(line, pair, half, 0), me.to_down, me.has_down)
            self.send(p, "own_pair", self.own(p, slice(None), 1), view(line, pair, slice(None), 1), me.to_pair)
        if k == 1:
            other = view(line, 1 - pair, half, 0)
            self.arrive(p, "first", other)
            self.send(p, "up0b", other, other, me.to_up, me.has_up)
            self.send(p, "down0b", other, other, me.to_down, me.has_down)
            self.send(p, "own_half", other, other, me.to_half)
        if 1 <= k < lines:
            for sign, kind, target, more, enough in (
                (-1, "up", me.to_up, me.has_up, line >= k),
                (1, "down", me.to_down, me.has_down, line < lines - k),
            ):
                source = line + sign * k
                item = view(source, pair, half, 1)
                self.arrive(p, ("single_" + kind, k), item, enough)
                if k + 1 < lines:
                    self.send(p, ("single_" + kind, k + 1), item, item, target, enough & more)
                self.send(p, (kind + "_half", k), item, item, me.to_half, enough)
        if 2 <= k <= lines:
            step = k - 1
            for sign, kind, target, more, enough in (
                (-1, "up", me.to_up, me.has_up, line >= step),
                (1, "down", me.to_down, me.has_down, line < lines - step),
            ):
                source = line + sign * step
                both = view(source, slice(None), half, 0)
                if step == 1:
                    self.arrive(p, kind + "0a", view(source, pair, half, 0), enough)
                    self.arrive(p, kind + "0b", view(source, 1 - pair, half, 0), enough)
                else:
                    self.arrive(p, (kind, step), both, enough)
                if step + 1 < lines:
                    self.send(p, (kind, step + 1), both, both, target, enough & more)
                self.send(p, (kind + "_far", step), both, both, me.to_half, enough)
                self.arrive(p, (kind + "_half", step), view(source, pair, 1 - half, 1), enough)
                item = view(source, pair, slice(None), 1)
                self.send(p, (kind + "_pair", step), item, item, me.to_pair, enough)
        if k == lines + 1:
            self.arrive(p, "own_half", view(line, 1 - pair, 1 - half, 0))
            self.arrive(p, "own_pair", view(line, 1 - pair, slice(None), 1))
            for step in range(1, lines):
                for sign, kind, enough in ((-1, "up", line >= step), (1, "down", line < lines - step)):
                    source = line + sign * step
                    self.arrive(p, (kind + "_far", step), view(source, slice(None), 1 - half, 0), enough)
                    self.arrive(p, (kind + "_pair", step), view(source, 1 - pair, slice(None), 1), enough)
            self.local(p).wait()
            for step in range(1, me.tp_size):
                self.send(p, ("core", step), view(), view(), me.to_core(step))
        if k == lines + 2:
            for step in range(1, me.tp_size):
                sender = lax.rem(core - step + me.tp_size, me.tp_size)
                self.arrive(p, ("core", step), self.whole(p, sender))

    def stages(self):
        return self.place.lines + 3

    def finish(self):
        for copy, condition in self.pending:
            when(condition, copy.wait_send)


def greet_all(place):
    barrier = pltpu.get_barrier_semaphore()
    targets = [place.to_pair, place.to_half]
    targets += [place.to_core(step) for step in range(1, place.tp_size)]
    targets += [place.to_line(step) for step in range(1, place.lines)]
    for target in targets:
        pl.semaphore_signal(barrier, inc=1, device_id=target, device_id_type=MESH)
    pl.semaphore_wait(barrier, len(targets))


class Small:
    def __init__(self, place, own, whole, sems, slot):
        self.place, self.own, self.whole, self.sems, self.slot = place, own, whole, sems, slot
        self.copies = []

    def stage(self, k):
        me = self.place
        for copy in self.copies:
            copy.wait()
        first, targets, block = {
            0: (0, [me.to_pair], self.whole.at[me.core, me.fsdp]),
            1: (1, [me.to_line(step) for step in range(1, me.lines)], self.whole.at[me.core, pl.ds(me.line * 2, 2)]),
            2: (me.lines, [me.to_core(step) for step in range(1, me.tp_size)], self.whole.at[me.core]),
            3: (0, [], None),
        }[k]
        if k == 0:
            block[...] = self.own[...]
        self.copies = []
        for number, target in enumerate(targets):
            copy = copy_to(block, block, self.sems, self.slot + first + number, target)
            copy.start()
            self.copies.append(copy)


def gather_kernel(sizes, *refs):
    shards, (tokens, cotangent, small), refs = refs[:4], refs[4:7], refs[7:]
    wholes, (all_tokens, all_cotangent, all_small), refs = refs[:4], refs[4:7], refs[7:]
    send, recv, local_sems = refs
    place = Place(*sizes)
    greet_all(place)
    pieces = []
    for g, part, parts in ((0, 0, 1), (1, 0, 1), (2, 0, 2), (2, 1, 2), (3, 0, 2), (3, 1, 2)):
        per_core = shards[g].shape[-1]
        width = per_core // parts
        pieces.append((shards[g], wholes[g], part * width, width, per_core))
    gather = Gather(place, pieces, (send, recv), local_sems)
    extra = len(pieces) * gather.width
    small_gather = Small(place, small, all_small, (send, recv), extra + 2)
    exchanges = []
    half = place.half
    for number, (own, whole) in enumerate(((tokens, all_tokens), (cotangent, all_cotangent))):
        exchanges.append(copy_to(own.at[1 - half], whole.at[half], (send, recv), extra + number, place.to_half))
        exchanges.append(pltpu.make_async_copy(own.at[half], whole.at[half], local_sems.at[len(pieces) + number]))
    for slot in range(len(pieces) + gather.stages() - 1):
        for p in range(len(pieces)):
            if 0 <= slot - p < gather.stages():
                gather.stage(p, slot - p)
        if slot < 4:
            small_gather.stage(slot)
        if slot == 0:
            for copy in exchanges:
                copy.start()
    for copy in exchanges:
        copy.wait()
    gather.finish()


def gather_all(mesh, shards, tokens, cotangent, small):
    fsdp, ctx, tp = (mesh.shape[name] for name in ("fsdp", "ctx", "tp"))
    lines = fsdp // 2
    rows = shards[2].shape[0] // 4

    def split(shard):
        return shard.reshape(shard.shape[:-2] + (2, 2, rows, shard.shape[-1]))

    shards = [split(shard) for shard in shards]

    def whole(shard):
        return jax.ShapeDtypeStruct(shard.shape[:-4] + (lines, 2, 2, 2, rows, shard.shape[-1] * tp), BF)

    arrivals = 2 + 1 + lines - 1 + tp - 1
    count = 6 * Gather.slots(lines, tp) + arrivals
    vmem, hbm = pl.BlockSpec(memory_space=pltpu.VMEM), pl.BlockSpec(memory_space=pl.ANY)
    found = pl.pallas_call(
        functools.partial(gather_kernel, (fsdp, ctx, tp)),
        name="gather_weights",
        out_shape=[whole(shard) for shard in shards]
        + [jax.ShapeDtypeStruct(tokens.shape, BF)] * 2
        + [jax.ShapeDtypeStruct((tp, fsdp) + small.shape, small.dtype)],
        in_specs=[vmem] * 7,
        out_specs=[hbm] * 6 + [vmem],
        scratch_shapes=[
            pltpu.SemaphoreType.DMA((count,)),
            pltpu.SemaphoreType.DMA((count,)),
            pltpu.SemaphoreType.DMA((8,)),
        ],
        compiler_params=pltpu.CompilerParams(collective_id=0, has_side_effects=True),
    )(*shards, tokens, cotangent, small)
    return [one.reshape(one.shape[:-6] + (rows * 4 * fsdp, one.shape[-1])) for one in found[:4]] + list(found[4:])


class Scatter:
    KINDS = ("half0", "pair1", "half1", "pair0")

    def __init__(self, place, pieces, sems, local_sems):
        self.place, self.pieces, self.sems, self.local_sems = place, pieces, sems, local_sems
        lines = place.lines
        names = list(self.KINDS)
        for kind in ("up0", "down0", "up1", "down1"):
            names += [(kind, step) for step in range(1, lines)]
        names += [("core", step) for step in range(1, place.tp_size)]
        self.names = {name: number for number, name in enumerate(names)}
        self.width = len(names)
        self.pending = []

    @staticmethod
    def slots(lines, tp):
        return 4 + 4 * (lines - 1) + tp - 1

    @staticmethod
    def buffers(lead, lines, tp, rows, width):
        block = (rows, width)
        return [
            pltpu.VMEM((lead, lines, 2, 2, 2) + block, BF),
            pltpu.VMEM((tp - 1, lead, lines, 2, 2, 2) + block, BF),
            pltpu.VMEM((lead, lines, 2) + block, BF),
            pltpu.VMEM((lead, lines, 2) + block, BF),
            pltpu.VMEM((lead, lines) + block, BF),
            pltpu.VMEM((lead,) + block, BF),
            pltpu.VMEM((2, lines - 1, lead, 2) + block, BF),
            pltpu.VMEM((2, lines - 1, lead) + block, BF),
        ]

    def slot(self, piece, name):
        return piece * self.width + self.names[name]

    def send(self, piece, name, src, dst, target, condition=True):
        copy = copy_to(src, dst, self.sems, self.slot(piece, name), target)
        when(condition, copy.start)
        self.pending.append((copy, condition))

    def arrive(self, piece, name, dst, condition=True):
        copy = copy_to(dst, dst, self.sems, self.slot(piece, name), self.place.to_half)
        when(condition, copy.wait_recv)

    def add(self, sizes, into, found, condition=True):
        count = 1
        for size in sizes:
            count *= size

        def one(number, _):
            index = []
            for size in reversed(sizes):
                index.append(lax.rem(number, size))
                number = number // size
            index = tuple(reversed(index))
            here, there = into(*index), found(*index)
            here[...] = here[...] + there[...]
            return 0

        def run():
            lax.fori_loop(0, count, one, 0)

        when(condition, run)

    def grads(self, piece, core):
        grad, offset, width, per_core = self.pieces[piece][:4]
        columns = pl.ds(pl.multiple_of(core * per_core + offset, 128), width)
        return grad.at[(slice(None),) * (len(grad.shape) - 1) + (columns,)]

    def local(self, piece):
        total = self.pieces[piece][5]
        return pltpu.make_async_copy(self.grads(piece, self.place.core), total, self.local_sems.at[piece])

    def stage(self, p, k):
        me = self.place
        core, line, pair, half, lines = me.core, me.line, me.pair, me.half, me.lines
        out, total, cores, half0, pair1, half1, pair0, line0, line1 = self.pieces[p][4:]
        lead = total.shape[0]
        every = slice(None)
        if k == 0:
            self.local(p).start()
            for step in range(1, me.tp_size):
                target = lax.rem(core + step, me.tp_size)
                self.send(p, ("core", step), self.grads(p, target), cores.at[step - 1], me.to_core(step))
        if k == 1:
            self.local(p).wait()
            for step in range(1, me.tp_size):
                self.arrive(p, ("core", step), cores.at[step - 1])
                self.add(
                    (lead, lines, 2, 2, 2),
                    lambda *i: total.at[i],
                    lambda *i, step=step: cores.at[(step - 1,) + i],
                )
            self.send(p, "half0", total.at[:, :, :, 1 - half, 0], half0, me.to_half)
            self.send(p, "pair1", total.at[:, :, 1 - pair, :, 1], pair1, me.to_pair)
        if k == 2:
            self.arrive(p, "half0", half0)
            self.add((lead, lines, 2), lambda l, n, q: total.at[l, n, q, half, 0], lambda *i: half0.at[i])
            self.arrive(p, "pair1", pair1)
            self.add((lead, lines, 2), lambda l, n, q: total.at[l, n, pair, q, 1], lambda *i: pair1.at[i])
            self.send(p, "half1", total.at[:, :, pair, 1 - half, 1], half1, me.to_half)
        if k == 3:
            self.arrive(p, "half1", half1)
            self.add((lead, lines), lambda l, n: total.at[l, n, pair, half, 1], lambda *i: half1.at[i])
        for color, first, buffer in ((0, 2, line0), (1, 3, line1)):
            distance = lines - 1 - (k - first)
            if 1 <= distance + 1 <= lines - 1:
                d = distance + 1
                for way, sign, kind, enough in (
                    (0, -1, "up", (line >= 1) & (line - 1 + d < lines)),
                    (1, 1, "down", (line < lines - 1) & (line + 1 - d >= 0)),
                ):
                    about = line + sign - sign * d
                    self.arrive(p, (kind + str(color), d), buffer.at[way, d - 1], enough)
                    if color == 0:
                        self.add(
                            (lead, 2),
                            lambda l, q, about=about: total.at[l, about, q, half, 0],
                            lambda l, q, way=way, d=d: line0.at[way, d - 1, l, q],
                            enough,
                        )
                    else:
                        self.add(
                            (lead,),
                            lambda l, about=about: total.at[l, about, pair, half, 1],
                            lambda l, way=way, d=d: line1.at[way, d - 1, l],
                            enough,
                        )
            if 1 <= distance <= lines - 1:
                d = distance
                for way, sign, kind, target, enough in (
                    (0, -1, "up", me.to_up, line + d < lines),
                    (1, 1, "down", me.to_down, line - d >= 0),
                ):
                    about = line - sign * d
                    src = total.at[:, about, :, half, 0] if color == 0 else total.at[:, about, pair, half, 1]
                    self.send(p, (kind + str(color), d), src, buffer.at[way, d - 1], target, enough)
        if k == lines + 1:
            self.send(p, "pair0", total.at[:, line, 1 - pair, half, 0], pair0, me.to_pair)
        if k == lines + 2:
            self.arrive(p, "pair0", pair0)
            for l in range(lead):
                out[l, 0] = total[l, line, pair, half, 0].astype(F32) + pair0[l].astype(F32)
                out[l, 1] = total[l, line, pair, half, 1].astype(F32)

    def stages(self):
        return self.place.lines + 3

    def finish(self):
        for copy, condition in self.pending:
            when(condition, copy.wait_send)


def all_sum(place, values, buffers, sems, slot):
    pending = []

    def send(number, target, condition=True):
        copy = copy_to(values, buffers.at[number], sems, slot + number, target)
        when(condition, copy.start)
        return copy

    number = 0
    for targets in (
        [place.to_core(step) for step in range(1, place.tp_size)],
        [place.to_half],
        [place.to_pair],
        [place.to_line(step) for step in range(1, place.lines)],
    ):
        copies = [send(number + i, target) for i, target in enumerate(targets)]
        for copy in copies:
            copy.wait()
        for i in range(len(targets)):
            values[...] = values[...] + buffers[number + i]
        number += len(targets)


def scatter_kernel(sizes, *refs):
    grads, refs = refs[:4], refs[4:]
    (sums_in, *results), refs = refs[:3], refs[3:]
    outs, refs = refs[:4], refs[4:]
    (sums, *placed), refs = refs[:3], refs[3:]
    buffers, refs = refs[: 6 * 8], refs[6 * 8 :]
    sum_buffers, send, recv, local_sems = refs
    place = Place(*sizes)
    tp = place.tp_size
    greet_all(place)
    pieces = []
    for p, (g, part, parts) in enumerate(((0, 0, 1), (1, 0, 1), (2, 0, 2), (2, 1, 2), (3, 0, 2), (3, 1, 2))):
        per_core = grads[g].shape[-1] // tp
        width = per_core // parts
        out = outs[g].at[:, :, :, pl.ds(part * width, width)]
        pieces.append((grads[g], part * width, width, per_core, out) + tuple(buffers[8 * p : 8 * p + 8]))
    pieces = [pieces[p] for p in (4, 5, 2, 3, 1, 0)]
    scatter = Scatter(place, pieces, (send, recv), local_sems)
    sums[...] = sums_in[...]
    exchanges = []
    extra, half = len(pieces) * scatter.width, place.half
    for number, (own, whole) in enumerate(zip(results, placed)):
        exchanges.append(copy_to(own.at[1 - half], whole.at[half], (send, recv), extra + number, place.to_half))
        exchanges.append(pltpu.make_async_copy(own.at[half], whole.at[half], local_sems.at[len(pieces) + number]))
    for copy in exchanges:
        copy.start()
    for slot in range(len(pieces) + scatter.stages() - 1):
        for p in range(len(pieces)):
            if 0 <= slot - p < scatter.stages():
                scatter.stage(p, slot - p)
        if slot == 1:
            all_sum(place, sums, sum_buffers, (send, recv), extra + 2)
    for copy in exchanges:
        copy.wait()
    scatter.finish()


def scatter_all(mesh, grad_qkv, grad_out, grad_one, grad_two, sums, outputs, input_grad):
    fsdp, ctx, tp = (mesh.shape[name] for name in ("fsdp", "ctx", "tp"))
    lines = fsdp // 2
    rows = grad_one.shape[-2] // (8 * lines)

    def split(grad):
        return grad.reshape(grad.shape[:1] + (lines, 2, 2, 2, rows, grad.shape[-1]))

    grads = [split(grad) for grad in (grad_qkv, grad_out, grad_one, grad_two)]

    def part(grad):
        return jax.ShapeDtypeStruct((grad.shape[0], 2, rows, grad.shape[-1] // tp), F32)

    scratch = []
    for lead, width in (
        (3, grad_qkv.shape[-1] // tp),
        (1, grad_out.shape[-1] // tp),
        (1, grad_one.shape[-1] // tp // 2),
        (1, grad_one.shape[-1] // tp // 2),
        (1, grad_two.shape[-1] // tp // 2),
        (1, grad_two.shape[-1] // tp // 2),
    ):
        scratch += Scatter.buffers(lead, lines, tp, rows, width)
    arrivals = tp - 1 + 2 + lines - 1
    count = 6 * Scatter.slots(lines, tp) + arrivals + 2
    vmem, hbm = pl.BlockSpec(memory_space=pltpu.VMEM), pl.BlockSpec(memory_space=pl.ANY)
    found = pl.pallas_call(
        functools.partial(scatter_kernel, (fsdp, ctx, tp)),
        name="scatter_gradients",
        out_shape=[part(grad) for grad in grads]
        + [jax.ShapeDtypeStruct(sums.shape, F32)]
        + [jax.ShapeDtypeStruct(outputs.shape, BF)] * 2,
        in_specs=[hbm] * 4 + [vmem] * 3,
        out_specs=[vmem] * 5 + [hbm] * 2,
        scratch_shapes=scratch
        + [
            pltpu.VMEM((arrivals,) + sums.shape, F32),
            pltpu.SemaphoreType.DMA((count,)),
            pltpu.SemaphoreType.DMA((count,)),
            pltpu.SemaphoreType.DMA((8,)),
        ],
        compiler_params=pltpu.CompilerParams(collective_id=1, has_side_effects=True, vmem_limit_bytes=67043328),
    )(*grads, sums, outputs, input_grad)
    return [one.reshape(one.shape[0], 2 * rows, one.shape[-1]) for one in found[:4]] + list(found[4:])


SEQ_LEN = 577
HD = 64


def normalize_rows(values, gain_row, shift_row):
    average = jnp.mean(values, axis=-1, keepdims=True)
    centred = values - average
    inv_std = lax.rsqrt(jnp.mean(centred * centred, axis=-1, keepdims=True) + 1e-05)
    normed = centred * inv_std
    return normed, inv_std, normed * gain_row + shift_row


def normalize_back(upstream, normed, inv_std, gain_row):
    scaled = upstream * gain_row
    inner = (
        scaled
        - jnp.mean(scaled, axis=-1, keepdims=True)
        - normed * jnp.mean(scaled * normed, axis=-1, keepdims=True)
    )
    return inv_std * inner


def dot(form, left, right):
    return jnp.einsum(form, left, right, preferred_element_type=F32)


def body(mesh, inputs, cotangent, slot_mask, key_mask, ln1_gain, ln1_bias, w_qkv, b_qv, w_out, b_out, ln2_gain, ln2_bias, w_fc1, b_fc1, w_fc2, b_fc2):
    fsdp, ctx, tp = (mesh.shape[name] for name in ("fsdp", "ctx", "tp"))
    width = inputs.shape[-1]
    seq = inputs.shape[2] * ctx
    heads = width // HD
    half, core = lax.axis_index("ctx"), lax.axis_index("tp")
    vectors = (ln1_gain, ln1_bias, ln2_gain, ln2_bias, b_out, b_fc2, b_qv, b_fc1)
    small = jnp.concatenate([vector.reshape(-1) for vector in vectors]).astype(F32)
    small = jnp.pad(small, (0, -small.size % 1024)).reshape(-1, 128)
    found = gather_all(
        mesh, (w_qkv.transpose(1, 0, 2), w_out.T, w_fc1, w_fc2.T), inputs[:, 0], cotangent[:, 0], small
    )
    m_qkv, m_out, m_one, m_two, tokens, cotangents, all_small = found
    tokens, cotangents = tokens.reshape(seq, width), cotangents.reshape(seq, width)
    all_small = all_small.reshape(tp, fsdp, -1)
    whole, place = [], 0
    for vector in vectors:
        part = all_small[:, :, place : place + vector.size].reshape((tp, fsdp) + vector.shape)
        place += vector.size
        if vector.ndim == 1:
            whole.append(part[0].reshape(-1))
        elif vector.ndim == 2:
            whole.append(part.transpose(0, 2, 1, 3).reshape(-1))
        else:
            whole.append(part.transpose(2, 0, 3, 1, 4).reshape(2, -1))
    gain_one, shift_one, gain_two, shift_two, bias_out, bias_fc2, bias_qv, bias_fc1 = whole
    keys_ok = lax.dynamic_slice(key_mask, (half, core, 0), (1, 1, seq)).reshape(seq) > 0
    slot_ok = lax.dynamic_slice(slot_mask, (half, 0), (1, 1)).reshape(()) > 0
    rows_ok = ((jnp.arange(seq) < SEQ_LEN) & slot_ok).astype(F32)[:, None]

    rows_in = tokens.astype(F32)
    normed_one, inv_one, scaled_one = normalize_rows(rows_in, gain_one, shift_one)
    low_one = scaled_one.astype(BF)
    query = (dot("rd,de->re", low_one, m_qkv[0]) + bias_qv[0]).astype(BF).reshape(seq, heads, HD)
    keys = dot("rd,de->re", low_one, m_qkv[1]).astype(BF).reshape(seq, heads, HD)
    values = (dot("rd,de->re", low_one, m_qkv[2]) + bias_qv[1]).astype(BF).reshape(seq, heads, HD)
    scores = jnp.where(keys_ok[None, None, :], dot("qhd,khd->hqk", query, keys) * 0.125, -jnp.inf)
    row_max = jnp.max(scores, axis=-1, keepdims=True)
    lifted = jnp.exp(scores - row_max)
    row_sum = jnp.sum(lifted, axis=-1, keepdims=True)
    soft = lifted / row_sum
    soft_low = soft.astype(BF)
    mixed = dot("hqk,khd->qhd", soft_low, values).astype(BF).reshape(seq, width)
    hidden_one = rows_in + dot("re,de->rd", mixed, m_out) + bias_out
    normed_two, inv_two, scaled_two = normalize_rows(hidden_one, gain_two, shift_two)
    low_two = scaled_two.astype(BF)
    before = dot("rd,df->rf", low_two, m_one) + bias_fc1
    gate = jax.nn.sigmoid(1.702 * before)
    active = (before * gate).astype(BF)
    outputs = ((hidden_one + dot("rf,df->rd", active, m_two) + bias_fc2) * rows_ok).astype(BF)

    grad_out = cotangents.astype(F32) * rows_ok
    grad_low = grad_out.astype(BF)
    grad_two_matrix = dot("rd,rf->df", grad_low, active).astype(BF)
    grad_active = dot("rd,df->rf", grad_low, m_two)
    grad_before = (grad_active * (gate + 1.702 * before * gate * (1.0 - gate))).astype(BF)
    grad_one_matrix = dot("rd,rf->df", low_two, grad_before).astype(BF)
    grad_two = dot("rf,df->rd", grad_before, m_one)
    grad_hidden = grad_out + normalize_back(grad_two, normed_two, inv_two, gain_two)
    hidden_low = grad_hidden.astype(BF)
    grad_out_matrix = dot("rd,re->de", hidden_low, mixed).astype(BF)
    grad_mixed = dot("rd,de->re", hidden_low, m_out).astype(BF).reshape(seq, heads, HD)
    grad_soft = dot("qhd,khd->hqk", grad_mixed, values)
    inner_sum = jnp.sum(grad_soft * soft, axis=-1, keepdims=True)
    grad_scores = (soft * (grad_soft - inner_sum)).astype(BF)
    grad_query = (dot("hqk,khd->qhd", grad_scores, keys) * 0.125).astype(BF).reshape(seq, width)
    grad_keys = (dot("hqk,qhd->khd", grad_scores, query) * 0.125).astype(BF).reshape(seq, width)
    grad_values = dot("hqk,qhd->khd", soft_low, grad_mixed).astype(BF).reshape(seq, width)
    grad_qkv_matrix = jnp.stack([dot("rd,re->de", low_one, g).astype(BF) for g in (grad_query, grad_keys, grad_values)])
    grad_one = (
        dot("re,de->rd", grad_query, m_qkv[0])
        + dot("re,de->rd", grad_keys, m_qkv[1])
        + dot("re,de->rd", grad_values, m_qkv[2])
    )
    input_grad = (grad_hidden + normalize_back(grad_one, normed_one, inv_one, gain_one)).astype(BF)

    def over_rows(values):
        return jnp.sum(values.astype(F32), axis=0)

    sums = [
        over_rows(grad_one * normed_one),
        over_rows(grad_one),
        over_rows(grad_two * normed_two),
        over_rows(grad_two),
        over_rows(grad_hidden),
        over_rows(grad_out),
        over_rows(grad_query),
        over_rows(grad_values),
        over_rows(grad_before),
    ]
    found = scatter_all(
        mesh,
        grad_qkv_matrix,
        grad_out_matrix[None],
        grad_one_matrix[None],
        grad_two_matrix[None],
        jnp.concatenate(sums).reshape(-1, 128),
        outputs.reshape(ctx, -1, width),
        input_grad.reshape(ctx, -1, width),
    )
    s_qkv, s_out, s_one, s_two, sums, outputs, input_grad = found
    sums = sums.reshape(-1)
    device = lax.axis_index("fsdp") * ctx + half
    per = width // (fsdp * ctx * tp)
    own = lax.dynamic_slice(sums[: 6 * width].reshape(6, width), (0, (device * tp + core) * per), (6, per))
    bias_sums = sums[6 * width : 8 * width].reshape(2, heads, HD)
    b_qv_grad = lax.dynamic_slice(
        bias_sums, (0, core * (heads // tp), device * (HD // (fsdp * ctx))), (2, heads // tp, HD // (fsdp * ctx))
    )
    fc1_sums = sums[8 * width :].reshape(-1, 64)
    b_fc1_grad = lax.dynamic_slice(
        fc1_sums, (core * (fc1_sums.shape[0] // tp), device * (64 // (fsdp * ctx))), (fc1_sums.shape[0] // tp, 64 // (fsdp * ctx))
    )
    return (
        outputs[:, None],
        input_grad[:, None],
        own[0],
        own[1],
        s_qkv.transpose(1, 0, 2),
        b_qv_grad,
        s_out[0].T,
        own[4],
        own[2],
        own[3],
        s_one[0],
        b_fc1_grad,
        s_two[0].T,
        own[5],
    )


def solution(mesh):
    in_specs = (
        P(None, ("fsdp", "tp"), "ctx", None),
        P(None, ("fsdp", "tp"), "ctx", None),
        P(None, ("fsdp", "tp")),
        P(None, "fsdp", None),
        P("fsdp"),
        P("fsdp"),
        P("fsdp", None, "tp"),
        P(None, "tp", "fsdp"),
        P("tp", "fsdp"),
        P("fsdp"),
        P("fsdp"),
        P("fsdp"),
        P("fsdp", "tp"),
        P("tp", "fsdp"),
        P("tp", "fsdp"),
        P("fsdp"),
    )
    out_specs = (
        P(None, ("fsdp", "tp"), "ctx", None),
        P(None, ("fsdp", "tp"), "ctx", None),
        P(("fsdp", "ctx", "tp")),
        P(("fsdp", "ctx", "tp")),
        P(("fsdp", "ctx"), None, "tp"),
        P(None, "tp", ("fsdp", "ctx")),
        P("tp", ("fsdp", "ctx")),
        P(("fsdp", "ctx", "tp")),
        P(("fsdp", "ctx", "tp")),
        P(("fsdp", "ctx", "tp")),
        P(("fsdp", "ctx"), "tp"),
        P("tp", ("fsdp", "ctx")),
        P("tp", ("fsdp", "ctx")),
        P(("fsdp", "ctx", "tp")),
    )
    return jax.shard_map(
        functools.partial(body, mesh), mesh=mesh, in_specs=in_specs, out_specs=out_specs, check_vma=False
    )
```

time: 1210 us -> 563 us (0.47)
  waiting for transfers between devices: 616 us -> 0 us
  Pallas kernels: 0 us -> 295 us
  blocking collectives: 245 us -> 0 us
  local copies, waits for them, and re-layouts: 71.7 us -> 43.3 us
  other arithmetic: 60 us -> 38.1 us
  between operations: 18 us -> 1.83 us
  matrix products: 189 us -> 176 us
    pallas_call x0 -> x2, Pallas kernels: none -> 295 us  [the longest x1 166 us: scatter_all(): pl.pallas_call(functools.partial(scatter_kernel, (fsdp, ctx, tp)), name='...]
    reduce_scatter x12 -> x0, waiting for transfers between devices: 236 us -> none  [the longest x1 95.2 us: body(): lax.psum_scatter(grad_parts[3].astype(jnp.bfloat16), ('fsdp', 'ctx'), sca...]
    all_gather x16 -> x0, waiting for transfers between devices: 223 us -> none  [the longest x1 78.1 us: body(): lax.all_gather(w_fc2, 'fsdp', axis=1, tiled=True)]
    all_gather x8 -> x0, blocking collectives: 171 us -> none  [the longest x1 30.4 us: body(): lax.all_gather(b_qv, 'fsdp', axis=2, tiled=True)]
    unnamed x38 -> x0, waiting for transfers between devices: 157 us -> none
    unnamed x1 -> x0, blocking collectives: 73.3 us -> none
    unnamed x161 -> x108, local copies, waits for them, and re-layouts: 49.1 us -> 19 us
    dot_general x36 -> x23, matrix products: 189 us -> 161 us  [dot(): return jnp.einsum(form, left, right, preferred_element_type=F32)]
  transfers between devices with their start and end apart: 33 -> 0, of which waited for: 15 -> 0; matrix products, arithmetic and copies ran while one was open for 24% -> 0% of each run, Pallas kernels for 0% -> 0%
where the time goes in v1:
time: 563 us; the launch traced here: 554 us
  Pallas kernels  295 us (52%)
  matrix products  176 us (31%)
  local copies, waits for them, and re-layouts  43.3 us (8%)
  other arithmetic  38.1 us (7%)
    pallas_call x1, Pallas kernels, scatter_all(): pl.pallas_call(functools.partial(scatter_kernel, (fsdp, ctx, tp)), name='...  166 us
    dot_general x23, matrix products, dot(): return jnp.einsum(form, left, right, preferred_element_type=F32)  161 us
    pallas_call x1, Pallas kernels, gather_all(): pl.pallas_call(functools.partial(gather_kernel, (fsdp, ctx, tp)), name='g...  129 us
    convert_element_type x1, other arithmetic, body(): grad_scores = (soft * (grad_soft - inner_sum)).astype(BF)  20.8 us
    unnamed x108, local copies, waits for them, and re-layouts  19 us
    sub x1, matrix products, body(): lifted = jnp.exp(scores - row_max)  14.8 us

profile of v1, /device:TPU:0, one launch (start us, length us, event | category | flops | bytes accessed | tf_op | source)
XLA Modules:
  0.0 554.1 jit_solution(8806148121203853398)
XLA Ops:
  15.4 128.8 %gather_weights.1 = (bf16[3,4,2,2,2,32,1024]{6,5,4,3,2,1,0:T(8,128)(2,1)}, bf16[4,2,2,2,32,1024]{5,4,3,2,1,0:T(8,128)(2,1)}, bf16[4,2,2,2,32,4096]{5,4,3,2,1,0:T...) custom-call(bf16[3,2,2,32,512]{4,3,2,1,0:T(8,128)(2,1)} %bitcast.207, ...), custom_call_target="tpu_custom_call" | custom-call | tf_op jit(solution)/shard_map/gather_weights/pallas_call | solution.py:257
  146.1 3.4 fusion.17
  152.6 5.3 fusion.35
  164.1 4.5 add_convert_fusion.3
  171.0 3.8 convolution_convert_fusion.7
  176.5 14.8 %fusion.37 = (f32[16,592]{1,0:T(8,128)S(1)}, f32[16,592,592]{1,2,0:T(8,128)}) fusion(pred[592]{0:T(1024)(128)(4,1)S(1)} %compare_reduce_fusion, bf16[592,16,64]{0,2,1:T(8,128)(2,1)} %bitcast.165, bf16[592,16,64]{0,2,1:T(8,128)(2,1)S(1)} %bitcast.163), kind=kOutput, calls=%fused_computation.113 | convolution fusion | flops 740180544 | bytes 24893008 | tf_op jit(solution)/shard_map/sub | solution.py:598
  191.2 10.5 %fusion.19 = bf16[16,64,592]{2,1,0:T(8,128)(2,1)S(1)} fusion(bf16[592,16,64]{0,2,1:T(8,128)(2,1)} %bitcast.183, f32[16,592,592]{1,2,0:T(8,128)} %get-tuple-element.101, f32[16,592]{1,0:T(8,128)S(1)} %get-tuple-element.100), kind=kOutput, calls=%fused_computation.61 | convolution fusion | flops 729571328 | bytes 24892416 | tf_op jit(solution)/shard_map/hqk,khd->qhd/dot_general | solution.py:557
  202.8 4.0 bitcast_add_fusion
  207.5 7.8 %fusion.29 = f32[592,4096]{1,0:T(8,128)} fusion(bf16[1024,4096]{1,0:T(8,128)(2,1)S(1)} %bitcast.214, f32[1024]{0:T(1024)S(1)} %get-tuple-element.87, f32[1024]{0:T(1024)S(1)} %get-tuple-element.88, f32[592,1024]{1,0:T(8,128)S(1)} %bitcast_add_fusion, f32[592]{0:T(1024)S(1)} %add_rsqrt_fusion, f32[592]{0:T(1024)S(1)} %broadcast_multiply_fusion.4, ...), kind=kOutput, calls=%fused_computation.68 | convolution fusion | flops 4969693184 | bytes 20529792 | tf_op jit(solution)/shard_map/rd,df->rf/dot_general | solution.py:557
  215.3 12.2 %multiply_convert_fusion.5 = bf16[592,1024]{1,0:T(8,128)(2,1)} fusion(f32[592,1024]{1,0:T(8,128)S(1)} %bitcast_add_fusion, bf16[1024,4096]{1,0:T(8,128)(2,1)} %bitcast.215, f32[1024]{0:T(1024)S(1)} %get-tuple-element.86, f32[1024]{0:T(1024)S(1)} %get-tuple-element.89, f32[592]{0:T(1024)S(1)} %fusion.31, f32[592,4096]{1,0:T(8,128)} %fusion.29, ...), kind=kOutput, calls=%fused_computation.39 | convolution fusion | flops 4986060800 | bytes 21752128 | tf_op jit(solution)/shard_map/rf,df->rd/dot_general | solution.py:557
  227.5 10.1 %convert_reduce_fusion = (f32[4096]{0:T(1024)S(1)}, bf16[592,4096]{1,0:T(8,128)(2,1)S(1)}) fusion(f32[592,4096]{1,0:T(8,128)S(1)} %copy-done.35, f32[4096]{0:T(1024)S(1)} %add.167, bf16[592,1024]{1,0:T(8,128)(2,1)S(1)} %bitcast.188, bf16[1024,4096]{1,0:T(8,128)(2,1)} %bitcast.216), kind=kOutput, calls=%fused_computation.10 | convolution fusion | flops 4997574656 | bytes 24182784 | tf_op jit(solution)/shard_map/rd,df->rf/dot_general | solution.py:557
  237.7 10.1 %multiply_reduce_fusion.2 = (f32[1024]{0:T(1024)S(1)}, f32[592]{0:T(1024)S(1)}, f32[592]{0:T(1024)S(1)}, f32[1024]{0:T(1024)S(1)}, f32[592,1024]{1,0:T(8,128)S(1)}) fusion(f32[592]{0:T(1024)S(1)} %add_rsqrt_fusion, f32[592]{0:T(1024)S(1)} %broadcast_multiply_fusion.4, f32[592,1024]{1,0:T(8,128)S(1)} %bitcast_add_fusion, f32[1024]{0:T(1024)S(1)} %get-tuple-element.89, ...), kind=kOutput, calls=%fused_computation.40 | convolution fusion | flops 4972114944 | bytes 18113792 | tf_op jit(solution)/shard_map/rf,df->rd/dot_general | solution.py:557
  252.9 9.4 %convolution_convert_fusion = bf16[1024,4096]{1,0:T(8,128)(2,1)} fusion(bf16[592,1024]{1,0:T(8,128)(2,1)S(1)} %get-tuple-element.83, f32[592,4096]{1,0:T(8,128)S(1)} %bitcast.222, f32[4096]{0:T(1024)S(1)} %add.167), kind=kOutput, calls=%fused_computation.14 | convolution fusion | flops 4987224064 | bytes 19316736 | tf_op jit(solution)/shard_map/rd,rf->df/dot_general | solution.py:557
  264.6 4.7 convolution_convert_fusion.2
  269.3 11.8 %convolution_convert_fusion.1 = bf16[1024,4096]{1,0:T(8,128)(2,1)} fusion(bf16[592,4096]{1,0:T(8,128)(2,1)} %copy-done.36, f32[1024]{0:T(1024)S(1)} %get-tuple-element.87, f32[1024]{0:T(1024)S(1)} %get-tuple-element.88, f32[592,1024]{1,0:T(8,128)S(1)} %copy-done.3, f32[592]{0:T(1024)S(1)} %add_rsqrt_fusion, f32[592]{0:T(1024)S(1)} %broadcast_multiply_fusion.4, ...), kind=kOutput, calls=%fused_computation.15 | convolution fusion | flops 4973887488 | bytes 15680128 | tf_op jit(solution)/shard_map/rd,rf->df/dot_general | solution.py:557
  281.2 13.1 %convert_reduce_fusion.1 = (f32[16,64]{1,0:T(8,128)S(1)}, bf16[16,64,592]{2,1,0:T(8,128)(2,1)}) fusion(bf16[592,16,64]{0,2,1:T(8,128)(2,1)} %bitcast.185, f32[16,592,592]{1,2,0:T(8,128)} %get-tuple-element.101, f32[16,592]{1,0:T(8,128)S(1)} %get-tuple-element.100), kind=kOutput, calls=%fused_computation.21 | convolution fusion | flops 730782720 | bytes 24896512 | tf_op jit(solution)/shard_map/hqk,qhd->khd/dot_general | solution.py:557
  294.3 4.9 convolution_convert_fusion.3
  299.2 20.2 %multiply_reduce_fusion = (f32[16,592]{1,0:T(8,128)S(1)}, f32[16,592,592]{1,2,0:T(8,128)}) fusion(f32[16,592,592]{1,2,0:T(8,128)} %get-tuple-element.101, f32[16,592]{1,0:T(8,128)S(1)} %get-tuple-element.100, bf16[592,16,64]{0,2,1:T(8,128)(2,1)} %bitcast.186, bf16[592,16,64]{0,2,1:T(8,128)(2,1)} %bitcast.184), kind=kOutput, calls=%fused_computation.2 | convolution fusion | flops 734563072 | bytes 47360000 | tf_op jit(solution)/shard_map/qhd,khd->hqk/dot_general | solution.py:557
  319.4 20.8 %multiply_convert_fusion = bf16[16,592,592]{1,2,0:T(8,128)(2,1)} fusion(f32[16,592,592]{1,2,0:T(8,128)} %get-tuple-element.104, f32[16,592]{1,0:T(8,128)S(1)} %get-tuple-element.103, f32[16,592,592]{1,2,0:T(8,128)} %get-tuple-element.101, f32[16,592]{1,0:T(8,128)S(1)} %get-tuple-element.100), kind=kLoop, calls=%fused_computation.1 | loop fusion | flops 22429696 | bytes 56150016 | tf_op jit(solution)/shard_map/convert_element_type | solution.py:624
  340.2 9.3 %multiply_convert_fusion.3 = bf16[16,64,592]{2,1,0:T(8,128)(2,1)} fusion(bf16[592,16,64]{0,2,1:T(8,128)(2,1)S(1)} %bitcast.166, bf16[16,592,592]{1,2,0:T(8,128)(2,1)} %multiply_convert_fusion), kind=kOutput, calls=%fused_computation.23 | convolution fusion | flops 718962688 | bytes 13639680 | tf_op jit(solution)/shard_map/hqk,qhd->khd/dot_general | solution.py:557
  349.5 7.8 %convert_reduce_fusion.2 = (f32[16,64]{1,0:T(8,128)S(1)}, bf16[16,64,592]{2,1,0:T(8,128)(2,1)}) fusion(bf16[592,16,64]{0,2,1:T(8,128)(2,1)S(1)} %bitcast.164, bf16[16,592,592]{1,2,0:T(8,128)(2,1)} %multiply_convert_fusion), kind=kOutput, calls=%fused_computation.22 | convolution fusion | flops 720174080 | bytes 13643776 | tf_op jit(solution)/shard_map/hqk,khd->qhd/dot_general | solution.py:557
  357.3 3.8 fusion.39
  373.0 3.3 pad_maximum_fusion.refs_0_
  376.3 166.2 %scatter_gradients.1 = (f32[3,2,32,512]{3,2,1,0:T(8,128)}, f32[1,2,32,512]{3,2,1,0:T(8,128)}, f32[1,2,32,2048]{3,2,1,0:T(8,128)}, f32[1,2,32,2048]{3,2,1,0:T(8,1...) custom-call(bf16[3,4,2,2,2,32,1024]{6,5,4,3,2,1,0:T(8,128)(2,1)} %pad_maximum_fusion.refs_0_, ...), custom_call_target="tpu_custom_call" | custom-call | tf_op jit(solution)/shard_map/scatter_gradients/pallas_call | solution.py:514
  (173 shorter events, 61.8 us)
Async XLA Ops:
  145.3 4.9 copy-start.25
  150.7 7.2 %copy-start.19 = (bf16[2,296,1024]{2,1,0:T(8,128)(2,1)}, bf16[2,296,1024]{2,1,0:T(8,128)(2,1)S(1)}, u32[]{:S(2)}) copy-start(bf16[2,296,1024]{2,1,0:T(8,128)(2,1)S(1)} %fusion.14) | copy-start | bytes 3637252
  157.9 13.1 %copy-start.12 = (bf16[1,4,2,2,2,32,1024]{6,5,4,3,2,1,0:T(8,128)(2,1)}, bf16[1,4,2,2,2,32,1024]{6,5,4,3,2,1,0:T(8,128)(2,1)S(1)}, u32[]{:S(2)}) copy-start(bf16[1,4,2,2,2,32,1024]{6,5,4,3,2,1,0:T(8,128)(2,1)S(1)} %get-tuple-element.80) | copy-start | bytes 6291460
  176.4 14.8 %copy-start.7 = (bf16[592,1024]{0,1:T(8,128)(2,1)}, bf16[592,1024]{0,1:T(8,128)(2,1)S(1)}, u32[]{:S(2)}) copy-start(bf16[592,1024]{0,1:T(8,128)(2,1)S(1)} %copy.51) | copy-start | bytes 3637252
  201.8 5.7 %slice-start = ((s8[8388608]{0:T(1024)(128)(4,1)}), s8[4194304]{0:T(1024)(128)(4,1)S(1)}, s32[]{:S(2)}) async-start(s8[8388608]{0:T(1024)(128)(4,1)} %bitcast.212), calls=%async_computation | async-start | bytes 8388608
  202.8 4.7 slice-start.1
  206.8 41.1 %copy-start.2 = (f32[592,1024]{1,0:T(8,128)}, f32[592,1024]{1,0:T(8,128)S(1)}, u32[]{:S(2)}) copy-start(f32[592,1024]{1,0:T(8,128)S(1)} %bitcast_add_fusion) | copy-start | bytes 7274500
  215.3 12.2 %copy-start.17 = (bf16[2,296,1024]{2,1,0:T(8,128)(2,1)S(1)}, bf16[2,296,1024]{2,1,0:T(8,128)(2,1)}, u32[]{:S(2)}) copy-start(bf16[2,296,1024]{2,1,0:T(8,128)(2,1)} %get-tuple-element.85) | copy-start | bytes 3637252
  215.3 12.2 %copy-start.35 = (f32[592,4096]{1,0:T(8,128)S(1)}, f32[592,4096]{1,0:T(8,128)}, u32[]{:S(2)}) copy-start(f32[592,4096]{1,0:T(8,128)} %fusion.29) | copy-start | bytes 29097988
  237.7 10.1 %copy-start.36 = (bf16[592,4096]{1,0:T(8,128)(2,1)}, bf16[592,4096]{1,0:T(8,128)(2,1)S(1)}, u32[]{:S(2)}) copy-start(bf16[592,4096]{1,0:T(8,128)(2,1)S(1)} %get-tuple-element.111) | copy-start | bytes 14548996
  237.7 10.2 %copy-start.10 = (bf16[2,296,1024]{2,1,0:T(8,128)(2,1)S(1)}, bf16[2,296,1024]{2,1,0:T(8,128)(2,1)}, u32[]{:S(2)}) copy-start(bf16[2,296,1024]{2,1,0:T(8,128)(2,1)} %get-tuple-element.31) | copy-start | bytes 3637252
  247.9 4.0 slice-start.2
  247.9 4.0 slice-start.3
  249.4 3.4 slice-start.4
  264.6 4.7 copy-start.3
  319.3 20.8 %copy-start.9 = (bf16[592,1024]{0,1:T(8,128)(2,1)S(1)}, bf16[592,1024]{0,1:T(8,128)(2,1)}, u32[]{:S(2)}) copy-start(bf16[592,1024]{0,1:T(8,128)(2,1)} %copy.53) | copy-start | bytes 3637252
  340.2 9.3 %copy-start.8 = (bf16[592,1024]{0,1:T(8,128)(2,1)S(1)}, bf16[592,1024]{0,1:T(8,128)(2,1)}, u32[]{:S(2)}) copy-start(bf16[592,1024]{0,1:T(8,128)(2,1)} %copy-done.7) | copy-start | bytes 3637252
  357.3 3.8 copy-start.13
  357.3 3.8 copy-start.15
  542.5 7.0 %copy-start.18 = (bf16[2,296,1024]{2,1,0:T(8,128)(2,1)S(1)}, bf16[2,296,1024]{2,1,0:T(8,128)(2,1)}, u32[]{:S(2)}) copy-start(bf16[2,296,1024]{2,1,0:T(8,128)(2,1)} %get-tuple-element.36) | copy-start | bytes 3637252
  547.0 3.5 copy-start.23
  547.0 4.3 copy-start.24
  547.1 4.9 copy-start.22
  549.5 3.2 copy-start.21
  (18 other events, 35.8 us)
